TPU v7x, 32 devices: a whole 2x2x4 slice. The times are simulated.
32 devices in a mesh: dp: 8 (over y, x, core), seq: 4 (over z).
Axes of the slice: x: 2, y: 2, z: 4, core: 2. Of those that a mesh axis runs over, the one named last changes fastest.
Arguments:
- block_input: bfloat16 [2, 8, 1024, 768], P(None, 'dp', 'seq'), may hold values from -6 to 6
- cotangent: bfloat16 [2, 8, 1024, 768], P(None, 'dp', 'seq'), may hold values from -6 to 6
- segments: int32 [2, 8, 1024], P(None, 'dp'), may hold values from 0 to 3, never falling along the last dimension, each value on 1 to 768 neighbouring positions
- rand_blocks: int32 [12, 16, 3], replicated, may hold values from 0 to 15
- w_attn: float32 [768, 2304], P('dp'), may hold values from -0.21875 to 0.21875
- w_out: float32 [768, 768], P('dp'), may hold values from -1.5 to 1.5
- w_up: float32 [768, 3072], P('dp'), may hold values from -0.21875 to 0.21875
- w_down: float32 [3072, 768], P('dp'), may hold values from -0.109375 to 0.109375
- up_bias: float32 [3072], P('dp'), may hold values from -3 to 3
- bias_rows: float32 [6, 768], P(None, 'dp'), may hold values from -2 to 2
- norm_gains: float32 [2, 768], P(None, 'dp'), may hold values from 0.25 to 1.75
Outputs:
- block_output: bfloat16 [2, 8, 1024, 768], P(None, 'dp', 'seq')
- input_grad: float32 [2, 8, 1024, 768], P(None, 'dp', 'seq')
- grad_w_attn: float32 [768, 2304], P('dp')
- grad_w_out: float32 [768, 768], P('dp')
- grad_w_up: float32 [768, 3072], P('dp')
- grad_w_down: float32 [3072, 768], P('dp')
- grad_up_bias: float32 [3072], P('dp')
- grad_bias_rows: float32 [6, 768], P(None, 'dp')
- grad_norm_gains: float32 [2, 768], P(None, 'dp')
Inputs may be any that keep to these rules, and one draw needn't show every extreme that they name: `segments`: segment numbers never fall along a sequence. `rand_blocks`: block numbers within the sequence.
All inputs are finite; a program needn't handle non-finite values.
Results may differ from a plain program's by a relative error of at most 0.018.
Values may be sent and summed in bfloat16 or wider, within the bound.
No kernel may reach another device: no remote copies, remote signals or barrier semaphores. Data moves between devices by JAX's collectives and lax.ppermute only.
A program may use at most 192 MiB of HBM per device.

v0:
```python
import jax
import jax.numpy as jnp
from jax import lax
from jax.sharding import PartitionSpec as P

EPSILON = 1e-05
MASKED = -1e30


def layer_norm(tensor, gain_row, offset):
    centre = tensor - jnp.mean(tensor, axis=-1, keepdims=True)
    spread = jnp.mean(centre * centre, axis=-1, keepdims=True)
    return centre * lax.rsqrt(spread + EPSILON) * gain_row + offset


def gelu_exact(tensor):
    return jax.nn.gelu(tensor, approximate=False)


def col_sums(tensor):
    return jnp.sum(tensor.astype(jnp.float32), axis=0)


def outer_grad(left, right):
    return lax.dot_general(
        left, right, (((0,), (0,)), ((), ())), preferred_element_type=jnp.float32
    )


def times_transposed(left, right):
    return lax.dot_general(
        left, right, (((1,), (1,)), ((), ())), preferred_element_type=jnp.float32
    )


def cast_half(params):
    return tuple((member.astype(jnp.bfloat16) for member in params))


def visible_mask(rand_blocks, first_row, local_rows, seq_len):
    head_count = rand_blocks.shape[0]
    nblocks = rand_blocks.shape[1]
    block_len = seq_len // nblocks
    local_blocks = local_rows // block_len
    query_block = (first_row + jnp.arange(local_rows, dtype=jnp.int32)) // block_len
    key_block = jnp.arange(seq_len, dtype=jnp.int32) // block_len
    nearby = jnp.abs(query_block[:, None] - key_block[None, :]) <= 1
    global_q = (query_block == 0) | (query_block == nblocks - 1)
    global_k = (key_block == 0) | (key_block == nblocks - 1)
    always = nearby | global_q[:, None] | global_k[None, :]
    chosen = lax.dynamic_slice_in_dim(rand_blocks, first_row // block_len, local_blocks, 1)
    block_ids = jnp.arange(nblocks, dtype=jnp.int32)
    random_hit = jnp.any(chosen[:, :, :, None] == block_ids[None, None, None, :], axis=2)
    random_hit = jnp.broadcast_to(
        random_hit[:, :, None, :, None], (head_count, local_blocks, block_len, nblocks, block_len)
    )
    return always[None] | random_hit.reshape(head_count, local_rows, seq_len)


def score_block(query_heads, key_heads, allowed, score_scale):
    scores = (
        jnp.einsum("sqhd,skhd->shqk", query_heads, key_heads, preferred_element_type=jnp.float32)
        * score_scale
    )
    return jnp.where(allowed, scores, MASKED)


def forward_pass(tokens, seg_full, weights, mask_blocks, first_row):
    w_attn_b, w_out_b, w_up_b, w_down_b, up_bias_b, bias_b, gain_b = weights
    seq_count, local_rows, model_width = tokens.shape
    head_count = mask_blocks.shape[0]
    head_size = model_width // head_count
    score_scale = head_size ** (-0.5)
    bias_f = bias_b.astype(jnp.float32)
    gain_f = gain_b.astype(jnp.float32)
    row_data = tokens.reshape(-1, model_width)
    projected = jnp.dot(row_data, w_attn_b, preferred_element_type=jnp.float32)
    queries = (projected[:, :model_width] + bias_f[0]).astype(jnp.bfloat16)
    keys_loc = projected[:, model_width : 2 * model_width].astype(jnp.bfloat16)
    values_loc = (projected[:, 2 * model_width :] + bias_f[1]).astype(jnp.bfloat16)
    keys_full, values_full = (
        lax.all_gather(
            keys_loc.reshape(seq_count, local_rows, model_width), "seq", axis=1, tiled=True
        ),
        lax.all_gather(
            values_loc.reshape(seq_count, local_rows, model_width), "seq", axis=1, tiled=True
        ),
    )
    seq_len = keys_full.shape[1]
    query_heads = queries.reshape(seq_count, local_rows, head_count, head_size)
    key_heads = keys_full.reshape(seq_count, seq_len, head_count, head_size)
    value_heads = values_full.reshape(seq_count, seq_len, head_count, head_size)
    seg_local = lax.dynamic_slice_in_dim(seg_full, first_row, local_rows, 1)
    allowed = mask_blocks[None] & (seg_local[:, None, :, None] == seg_full[:, None, None, :])
    scores = score_block(query_heads, key_heads, allowed, score_scale)
    row_max = jnp.max(scores, axis=-1, keepdims=True)
    exponent = jnp.exp(scores - row_max)
    row_total = jnp.sum(exponent, axis=-1, keepdims=True)
    attn_probs = exponent / row_total
    log_total = row_max + jnp.log(row_total)
    probs_low = attn_probs.astype(jnp.bfloat16)
    mixture = jnp.einsum(
        "shqk,skhd->sqhd", probs_low, value_heads, preferred_element_type=jnp.float32
    )
    attended = mixture.reshape(-1, model_width).astype(jnp.bfloat16)
    branch = jnp.dot(attended, w_out_b, preferred_element_type=jnp.float32) + bias_f[2]
    first_norm, first_back = jax.vjp(
        layer_norm, row_data.astype(jnp.float32) + branch, gain_f[0], bias_f[4]
    )
    first_low = first_norm.astype(jnp.bfloat16)
    pre_act = jnp.dot(first_low, w_up_b, preferred_element_type=jnp.float32) + up_bias_b.astype(
        jnp.float32
    )
    act_float, gelu_back = jax.vjp(gelu_exact, pre_act)
    activation = act_float.astype(jnp.bfloat16)
    ffn_out = jnp.dot(activation, w_down_b, preferred_element_type=jnp.float32) + bias_f[3]
    result, second_back = jax.vjp(layer_norm, first_norm + ffn_out, gain_f[1], bias_f[5])
    stored = (
        row_data,
        query_heads,
        key_heads,
        value_heads,
        allowed,
        log_total,
        attended,
        first_low,
        activation,
        first_back,
        gelu_back,
        second_back,
    )
    return (result.astype(jnp.bfloat16).reshape(seq_count, local_rows, model_width), stored)


def backward_pass(stored, upstream, weights):
    w_attn_b, w_out_b, w_up_b, w_down_b, up_bias_b, bias_b, gain_b = weights
    (
        row_data,
        query_heads,
        key_heads,
        value_heads,
        allowed,
        log_total,
        attended,
        first_low,
        activation,
        first_back,
        gelu_back,
        second_back,
    ) = stored
    seq_count, local_rows, head_count, head_size = query_heads.shape
    seq_len = key_heads.shape[1]
    model_width = head_count * head_size
    score_scale = head_size ** (-0.5)
    grad_second, grad_gain_two, grad_shift_two = second_back(upstream)
    ffn_grad = grad_second.astype(jnp.bfloat16)
    grad_down = outer_grad(activation, ffn_grad)
    grad_bias_down = col_sums(ffn_grad)
    act_grad = times_transposed(ffn_grad, w_down_b)
    (pre_float,) = gelu_back(act_grad)
    pre_grad = pre_float.astype(jnp.bfloat16)
    grad_up = outer_grad(first_low, pre_grad)
    grad_up_bias = col_sums(pre_grad)
    first_grad = grad_second + times_transposed(pre_grad, w_up_b)
    grad_first, grad_gain_one, grad_shift_one = first_back(first_grad)
    branch_grad = grad_first.astype(jnp.bfloat16)
    grad_out = outer_grad(attended, branch_grad)
    grad_bias_out = col_sums(branch_grad)
    attended_grad = (
        times_transposed(branch_grad, w_out_b)
        .astype(jnp.bfloat16)
        .reshape(seq_count, local_rows, head_count, head_size)
    )
    scores = score_block(query_heads, key_heads, allowed, score_scale)
    attn_probs = jnp.exp(scores - log_total)
    prob_grad = jnp.einsum(
        "sqhd,skhd->shqk", attended_grad, value_heads, preferred_element_type=jnp.float32
    )
    row_dot = jnp.sum(prob_grad * attn_probs, axis=-1, keepdims=True)
    score_grad = (attn_probs * (prob_grad - row_dot)).astype(jnp.bfloat16)
    query_grad = (
        jnp.einsum("shqk,skhd->sqhd", score_grad, key_heads, preferred_element_type=jnp.float32)
        * score_scale
    ).astype(jnp.bfloat16)
    probs_low = attn_probs.astype(jnp.bfloat16)
    value_part = jnp.einsum(
        "shqk,sqhd->skhd", probs_low, attended_grad, preferred_element_type=jnp.float32
    )
    key_part = (
        jnp.einsum("shqk,sqhd->skhd", score_grad, query_heads, preferred_element_type=jnp.float32)
        * score_scale
    )
    key_grad, value_grad = (
        lax.psum_scatter(
            key_part.reshape(seq_count, seq_len, model_width).astype(jnp.bfloat16),
            "seq",
            scatter_dimension=1,
            tiled=True,
        ).astype(jnp.float32),
        lax.psum_scatter(
            value_part.reshape(seq_count, seq_len, model_width).astype(jnp.bfloat16),
            "seq",
            scatter_dimension=1,
            tiled=True,
        ).astype(jnp.float32),
    )
    key_low = key_grad.astype(jnp.bfloat16).reshape(-1, model_width)
    value_low = value_grad.astype(jnp.bfloat16).reshape(-1, model_width)
    query_low = query_grad.reshape(-1, model_width)
    proj_grad = jnp.concatenate([query_low, key_low, value_low], axis=1)
    grad_attn = outer_grad(row_data, proj_grad)
    input_grad = grad_first + times_transposed(proj_grad, w_attn_b)
    grad_biases = jnp.stack(
        [
            col_sums(query_low),
            col_sums(value_low),
            grad_bias_out,
            grad_bias_down,
            grad_shift_one,
            grad_shift_two,
        ]
    )
    grad_gains = jnp.stack([grad_gain_one, grad_gain_two])
    gradients = (grad_attn, grad_out, grad_up, grad_down, grad_up_bias, grad_biases, grad_gains)
    return (input_grad.reshape(seq_count, local_rows, model_width), gradients)


def body(
    block_input,
    cotangent,
    segments,
    rand_blocks,
    w_attn,
    w_out,
    w_up,
    w_down,
    up_bias,
    bias_rows,
    norm_gains,
):
    micro_count, seq_count, local_rows, model_width = block_input.shape
    seq_len = segments.shape[2]
    first_row = lax.axis_index("seq") * local_rows
    mask_blocks = visible_mask(rand_blocks, first_row, local_rows, seq_len)
    masters = (w_attn, w_out, w_up, w_down, up_bias, bias_rows, norm_gains)
    halves = cast_half(masters)
    totals = tuple(
        (
            (
                jnp.zeros((member.shape[0] * lax.axis_size("dp"),) + member.shape[1:], jnp.float32)
                if member.ndim == 1 or (member is not bias_rows and member is not norm_gains)
                else jnp.zeros(
                    (member.shape[0], member.shape[1] * lax.axis_size("dp")), jnp.float32
                )
            )
            for member in masters
        )
    )
    outputs = []
    in_grads = []
    for micro_index in range(micro_count):
        fwd_set = (
            lax.all_gather(halves[0], "dp", axis=0, tiled=True),
            lax.all_gather(halves[1], "dp", axis=0, tiled=True),
            lax.all_gather(halves[2], "dp", axis=0, tiled=True),
            lax.all_gather(halves[3], "dp", axis=0, tiled=True),
            lax.all_gather(halves[4], "dp", axis=0, tiled=True),
            lax.all_gather(halves[5], "dp", axis=1, tiled=True),
            lax.all_gather(halves[6], "dp", axis=1, tiled=True),
        )
        result, stored = forward_pass(
            block_input[micro_index], segments[micro_index], fwd_set, mask_blocks, first_row
        )
        outputs.append(result)
        back_set = (
            lax.all_gather(halves[0], "dp", axis=0, tiled=True),
            lax.all_gather(halves[1], "dp", axis=0, tiled=True),
            lax.all_gather(halves[2], "dp", axis=0, tiled=True),
            lax.all_gather(halves[3], "dp", axis=0, tiled=True),
            lax.all_gather(halves[4], "dp", axis=0, tiled=True),
            lax.all_gather(halves[5], "dp", axis=1, tiled=True),
            lax.all_gather(halves[6], "dp", axis=1, tiled=True),
        )
        upstream = cotangent[micro_index].reshape(-1, model_width).astype(jnp.float32)
        input_grad, gradients = backward_pass(stored, upstream, back_set)
        in_grads.append(input_grad)
        totals = tuple((total_part + grad_part for total_part, grad_part in zip(totals, gradients)))
    shards = (
        lax.psum_scatter(totals[0], "dp", scatter_dimension=0, tiled=True),
        lax.psum_scatter(totals[1], "dp", scatter_dimension=0, tiled=True),
        lax.psum_scatter(totals[2], "dp", scatter_dimension=0, tiled=True),
        lax.psum_scatter(totals[3], "dp", scatter_dimension=0, tiled=True),
        lax.psum_scatter(totals[4], "dp", scatter_dimension=0, tiled=True),
        lax.psum_scatter(totals[5], "dp", scatter_dimension=1, tiled=True),
        lax.psum_scatter(totals[6], "dp", scatter_dimension=1, tiled=True),
    )
    summed = (
        lax.psum(shards[0].astype(jnp.bfloat16), "seq").astype(jnp.float32),
        lax.psum(shards[1].astype(jnp.bfloat16), "seq").astype(jnp.float32),
        lax.psum(shards[2].astype(jnp.bfloat16), "seq").astype(jnp.float32),
        lax.psum(shards[3].astype(jnp.bfloat16), "seq").astype(jnp.float32),
        lax.psum(shards[4].astype(jnp.bfloat16), "seq").astype(jnp.float32),
        lax.psum(shards[5].astype(jnp.bfloat16), "seq").astype(jnp.float32),
        lax.psum(shards[6].astype(jnp.bfloat16), "seq").astype(jnp.float32),
    )
    return (
        jnp.stack(outputs, 0),
        jnp.stack(in_grads, 0),
        summed[0],
        summed[1],
        summed[2],
        summed[3],
        summed[4],
        summed[5],
        summed[6],
    )


def solution(mesh):
    return jax.shard_map(
        body,
        mesh=mesh,
        in_specs=(
            P(None, "dp", "seq", None),
            P(None, "dp", "seq", None),
            P(None, "dp", None),
            P(),
            P("dp", None),
            P("dp", None),
            P("dp", None),
            P("dp", None),
            P("dp"),
            P(None, "dp"),
            P(None, "dp"),
        ),
        out_specs=(
            P(None, "dp", "seq", None),
            P(None, "dp", "seq", None),
            P("dp", None),
            P("dp", None),
            P("dp", None),
            P("dp", None),
            P("dp"),
            P(None, "dp"),
            P(None, "dp"),
        ),
        check_vma=False,
    )
```

profile of v0, /device:TPU:0, one launch (start us, length us, event | category | flops | bytes accessed | tf_op | source)
XLA Modules:
  0.0 952.1 jit_solution(16371674868866285277)
XLA Ops:
  9.3 37.9 %all-gather.16.cloned.1.call-done = bf16[768,2304]{1,0:T(8,128)(2,1)} async-done(((bf16[96,2304]{1,0:T(8,128)(2,1)}), bf16[768,2304]{1,0:T(8,128)(2,1)}) %all-gather.16.cloned.1.call-update) | async-done | bytes 3538960 | tf_op jit(solution)/shard_map/all_gather | solution.py:263
  47.2 3.2 fusion.64
  52.7 8.9 all-gather.4
  61.7 3.2 fusion.67
  72.5 7.9 all-gather.5
  80.5 8.8 all-gather.6
  89.6 4.3 broadcast_in_dim.25
  93.9 17.3 %reshape.625 = pred[12,256,1024]{2,1,0:T(32,128)(4,1)} reshape(pred[12,4,64,16,64]{4,3,2,1,0:T(8,128)(4,1)} %broadcast_in_dim.25) | data formatting | bytes 6291456 | tf_op jit(solution)/shard_map/reshape | solution.py:57
  115.5 6.6 fusion.100
  122.1 4.6 copy-done.2
  131.0 6.7 fusion.38
  137.7 15.0 %all-gather.18.cloned.1.call-done = bf16[768,768]{1,0:T(8,128)(2,1)} async-done(((bf16[96,768]{1,0:T(8,128)(2,1)}), bf16[768,768]{1,0:T(8,128)(2,1)}) %all-gather.18.cloned.1.call-update) | async-done | bytes 1179664 | tf_op jit(solution)/shard_map/all_gather | solution.py:264
  154.8 39.1 %all-gather.20.cloned.1.call-done = bf16[768,3072]{1,0:T(8,128)(2,1)} async-done(((bf16[96,3072]{1,0:T(8,128)(2,1)}), bf16[768,3072]{1,0:T(8,128)(2,1)}) %all-gather.20.cloned.1.call-update) | async-done | bytes 4718608 | tf_op jit(solution)/shard_map/all_gather | solution.py:265
  194.0 11.6 %multiply_convert_fusion.4 = (bf16[256,3072]{1,0:T(8,128)(2,1)}, f32[256,3072]{1,0:T(8,128)}, f32[256,3072]{1,0:T(8,128)}) fusion(f32[3072]{0:T(1024)S(1)} %bitcast.239, bf16[768,3072]{1,0:T(8,128)(2,1)} %all-gather.20.cloned.1.call-done, f32[256,768]{1,0:T(8,128)S(1)} %get-tuple-element.135, f32[256]{0:T(256)S(1)} %fusion.79, ...), kind=kOutput, calls=%fused_computation.37 | convolution fusion | flops 1260847104 | bytes 13389824 | tf_op jit(solution)/shard_map/dot_general | solution.py:111
  205.6 29.6 %all-gather.22.cloned.1.call-done = bf16[3072,768]{1,0:T(8,128)(2,1)} async-done(((bf16[384,768]{1,0:T(8,128)(2,1)}), bf16[3072,768]{1,0:T(8,128)(2,1)}) %all-gather.22.cloned.1.call-update) | async-done | bytes 4718608 | tf_op jit(solution)/shard_map/all_gather | solution.py:266
  235.2 4.3 fusion.102
  239.6 34.9 %all-gather.26.cloned.1.call-done = bf16[1024,768]{1,0:T(8,128)(2,1)} async-done(((bf16[256,768]{1,0:T(8,128)(2,1)}), bf16[1024,768]{1,0:T(8,128)(2,1)}) %all-gather.26.cloned.1.call-update) | async-done | bytes 1572880 | tf_op jit(solution)/shard_map/all_gather | solution.py:82
  277.4 6.8 fusion.97
  288.7 23.9 %all-gather.24.cloned.1.call-done = bf16[1024,768]{1,0:T(8,128)(2,1)} async-done(((bf16[256,768]{1,0:T(8,128)(2,1)}), bf16[1024,768]{1,0:T(8,128)(2,1)}) %all-gather.24.cloned.1.call-update) | async-done | bytes 1572880 | tf_op jit(solution)/shard_map/all_gather | solution.py:85
  315.2 6.6 fusion.39
  322.7 11.6 %multiply_convert_fusion.5 = (bf16[256,3072]{1,0:T(8,128)(2,1)S(1)}, f32[256,3072]{1,0:T(8,128)S(1)}, f32[256,3072]{1,0:T(8,128)}) fusion(f32[3072]{0:T(1024)S(1)} %bitcast.240, bf16[768,3072]{1,0:T(8,128)(2,1)} %all-gather.20.cloned.1.call-done, f32[256,768]{1,0:T(8,128)S(1)} %get-tuple-element.128, f32[768]{0:T(1024)S(1)} %get-tuple-element.70, ...), kind=kOutput, calls=%fused_computation.50 | convolution fusion | flops 1260847104 | bytes 13389824 | tf_op jit(solution)/shard_map/dot_general | solution.py:111
  352.8 8.1 fusion.24
  361.0 7.0 multiply_reduce_fusion.1
  368.0 6.4 multiply_convert_fusion.1
  383.4 8.0 fusion.27
  391.5 7.2 multiply_reduce_fusion
  398.6 6.5 multiply_convert_fusion
  413.2 6.2 convert_reduce_fusion.7
  419.4 5.7 convert_reduce_fusion.11
  425.1 6.5 reduce-scatter.17.cloned.1.call-done
  431.6 5.2 fusion.60
  436.9 31.9 %reduce-scatter.23.cloned.1.call-done = bf16[1,256,768]{1,2,0:T(8,128)(2,1)} async-done(((bf16[1,1024,768]{1,2,0:T(8,128)(2,1)}), bf16[1,256,768]{1,2,0:T(8,128)(2,1)}) %reduce-scatter.23.cloned.1.call-update) | async-done | bytes 393232 | tf_op jit(solution)/shard_map/reduce_scatter | solution.py:200
  468.8 36.4 %reduce-scatter.21.cloned.1.call-done = bf16[1,256,768]{1,2,0:T(8,128)(2,1)} async-done(((bf16[1,1024,768]{1,2,0:T(8,128)(2,1)}), bf16[1,256,768]{1,2,0:T(8,128)(2,1)}) %reduce-scatter.21.cloned.1.call-update) | async-done | bytes 393232 | tf_op jit(solution)/shard_map/reduce_scatter | solution.py:194
  505.2 7.4 add_bitcast_fusion
  512.6 8.2 copy.84
  520.9 3.1 fusion.87
  524.1 5.2 convolution_add_fusion.1
  533.2 5.2 convolution_add_fusion
  541.6 8.5 reduce-scatter.25.cloned.1.call-done
  551.7 67.7 %reduce-scatter.31.cloned.1.call-done = f32[96,2304]{1,0:T(8,128)} async-done(((f32[768,2304]{1,0:T(8,128)}), f32[96,2304]{1,0:T(8,128)}) %reduce-scatter.31.cloned.1.call-update) | async-done | bytes 884752
  621.6 77.6 %reduce-scatter.27.cloned.1.call-done = f32[96,3072]{1,0:T(8,128)} async-done(((f32[768,3072]{1,0:T(8,128)}), f32[96,3072]{1,0:T(8,128)}) %reduce-scatter.27.cloned.1.call-update) | async-done | bytes 1179664 | tf_op jit(solution)/shard_map/reduce_scatter | solution.py:291
  701.4 77.7 %reduce-scatter.29.cloned.1.call-done = f32[384,768]{1,0:T(8,128)} async-done(((f32[3072,768]{1,0:T(8,128)}), f32[384,768]{1,0:T(8,128)}) %reduce-scatter.29.cloned.1.call-update) | async-done | bytes 1179664 | tf_op jit(solution)/shard_map/reduce_scatter | solution.py:292
  782.5 23.1 %all-reduce = bf16[3072]{0:T(1024)(128)(2,1)S(1)} all-reduce(f32[3072]{0:T(1024)S(1)} %add.337), channel_id=14, replica_groups=mesh['dp'=8,'seq'=4] {'dp'}, use_global_device_ids=true, to_apply=%region_37.38.clone | all-reduce | flops 3072 | bytes 18432
  806.7 9.8 %reduce-scatter.35.cloned.1.call-done = f32[96,2]{1,0:T(8,128)} async-done(((f32[768,2]{1,0:T(8,128)}), f32[96,2]{1,0:T(8,128)}) %reduce-scatter.35.cloned.1.call-update) | async-done | bytes 784
  817.4 3.3 fusion.32
  823.2 30.0 %reduce-scatter.33.cloned.1.call-done = f32[96,6]{1,0:T(8,128)} async-done(((f32[768,6]{1,0:T(8,128)}), f32[96,6]{1,0:T(8,128)}) %reduce-scatter.33.cloned.1.call-update) | async-done | bytes 2320
  854.1 11.8 %all-reduce.1 = (bf16[384]{0:T(512)(128)(2,1)S(1)}, bf16[6,96]{1,0:T(8,128)(2,1)S(1)}, bf16[2,96]{1,0:T(2,128)(2,1)S(1)}) all-reduce(bf16[384]{0:T(512)(128)(2,1)S(1)} %dynamic-slice.5, bf16[6,96]{1,0:T(8,128)(2,1)S(1)} %copy.87, bf16[2,96]{1,0:T(2,128)(2,1)S(1)} %copy.89), channel_id=1, replica_groups=mesh['dp'=8,'seq'=4] {'seq'}, use_global_device_ids=true, to_apply=%region_38.39 | all-reduce | flops 1152 | bytes 4608 | tf_op jit(solution)/shard_map/psum | solution.py:302
  867.7 70.5 %all-reduce.5.cloned.1.call-done = (bf16[96,2304]{0,1:T(8,128)(2,1)}, bf16[96,768]{1,0:T(8,128)(2,1)}, bf16[96,3072]{1,0:T(8,128)(2,1)}, bf16[384,768]{1,0:T(8,128)(2,1)}) async-done(((bf16[96,2304]{0,1:T(8,128)(2,1)}, bf16[96,768]{1,0:T(8,128)(2,1)}, bf16[96,3072]{1,0:T(8,128)(2,1)}, bf16[384,768]{1,0:T(8,128)(2,1)}), (bf16[96,2304]{0,1:T(8,128)(2,1)}, bf16[96,768]{1,0:T(8,128)(2,1)}, ...) | async-done | bytes 1769488 | tf_op jit(solution)/shard_map/psum | solution.py:298
  (290 shorter events, 98.7 us)
Async XLA Ops:
  7.2 82.2 %copy-start = (s32[12,16,3]{1,2,0:T(4,128)S(1)}, s32[12,16,3]{1,2,0:T(4,128)}, u32[]{:S(2)}) copy-start(s32[12,16,3]{1,2,0:T(4,128)} %param.14) | copy-start | bytes 6916
  7.2 40.0 %all-gather.16.cloned.1.call-start = ((), (), s32[]{:S(2)}) async-start(), calls=%async_computation.10 | async-start | bytes 3981312 | tf_op jit(solution)/shard_map/all_gather | solution.py:263
  9.2 43.4 %copy-start.50 = (f32[6,96]{1,0:T(8,128)S(1)}, f32[6,96]{1,0:T(8,128)}, u32[]{:S(2)}) copy-start(f32[6,96]{1,0:T(8,128)} %param.20) | copy-start | bytes 6916
  9.3 52.5 %copy-start.19 = (bf16[2,1,256,768]{3,2,1,0:T(8,128)(2,1)S(1)}, bf16[2,1,256,768]{3,2,1,0:T(8,128)(2,1)}, u32[]{:S(2)}) copy-start(bf16[2,1,256,768]{3,2,1,0:T(8,128)(2,1)} %param.11) | copy-start | bytes 2359300
  9.3 104.4 %all-gather.30.cloned.1.call-start = ((), (), s32[]{:S(2)}) async-start(), calls=%async_computation.24 | async-start | bytes 1966080 | tf_op jit(solution)/shard_map/all_gather | solution.py:82
  52.6 76.6 %all-gather.28.cloned.1.call-start = ((), (), s32[]{:S(2)}) async-start(), calls=%async_computation.23 | async-start | bytes 1966080 | tf_op jit(solution)/shard_map/all_gather | solution.py:85
  66.3 86.4 %all-gather.18.cloned.1.call-start = ((), (), s32[]{:S(2)}) async-start(), calls=%async_computation.11 | async-start | bytes 1327104 | tf_op jit(solution)/shard_map/all_gather | solution.py:264
  67.1 126.9 %all-gather.20.cloned.1.call-start = ((), (), s32[]{:S(2)}) async-start(), calls=%async_computation.12 | async-start | bytes 5308416 | tf_op jit(solution)/shard_map/all_gather | solution.py:265
  69.3 165.9 %all-gather.22.cloned.1.call-start = ((), (), s32[]{:S(2)}) async-start(), calls=%async_computation.13 | async-start | bytes 5308416 | tf_op jit(solution)/shard_map/all_gather | solution.py:266
  71.6 202.9 %all-gather.26.cloned.1.call-start = ((), (), s32[]{:S(2)}) async-start(), calls=%async_computation.22 | async-start | bytes 1966080 | tf_op jit(solution)/shard_map/all_gather | solution.py:82
  72.4 240.2 %all-gather.24.cloned.1.call-start = ((), (), s32[]{:S(2)}) async-start(), calls=%async_computation.21 | async-start | bytes 1966080 | tf_op jit(solution)/shard_map/all_gather | solution.py:85
  93.9 17.4 %copy-start.49 = (s32[2,1,1024]{2,1,0:T(1,128)S(1)}, s32[2,1,1024]{2,1,0:T(1,128)}, u32[]{:S(2)}) copy-start(s32[2,1,1024]{2,1,0:T(1,128)} %param.13) | copy-start | bytes 24580
  112.9 9.1 copy-start.46
  113.1 8.9 copy-start.15
  113.3 164.0 %copy-start.17 = (bf16[256,768]{0,1:T(8,128)(2,1)}, bf16[256,768]{0,1:T(8,128)(2,1)S(1)}, u32[]{:S(2)}) copy-start(bf16[256,768]{0,1:T(8,128)(2,1)S(1)} %copy.75) | copy-start | bytes 1179652
  113.3 311.8 %reduce-scatter.19.cloned.1.call-start = ((), (), s32[]{:S(2)}) async-start(), calls=%async_computation.15 | async-start | bytes 1966080 | tf_op jit(solution)/shard_map/reduce_scatter | solution.py:200
  115.4 6.6 copy-start.10
  131.0 6.7 copy-start.12
  131.0 21.7 %copy-start.20 = (bf16[2,1,256,768]{3,2,1,0:T(8,128)(2,1)S(1)}, bf16[2,1,256,768]{3,2,1,0:T(8,128)(2,1)}, u32[]{:S(2)}) copy-start(bf16[2,1,256,768]{3,2,1,0:T(8,128)(2,1)} %param.11) | copy-start | bytes 2359300
  137.7 67.9 %copy-start.44 = (bf16[12,64,256]{2,1,0:T(8,128)(2,1)}, bf16[12,64,256]{2,1,0:T(8,128)(2,1)S(1)}, u32[]{:S(2)}) copy-start(bf16[12,64,256]{2,1,0:T(8,128)(2,1)S(1)} %fusion.38) | copy-start | bytes 1179652
  239.6 37.8 %copy-start.47 = (pred[256,1024]{1,0:T(8,128)(4,1)S(1)}, pred[256,1024]{1,0:T(8,128)(4,1)}, u32[]{:S(2)}) copy-start(pred[256,1024]{1,0:T(8,128)(4,1)} %copy-done.46) | copy-start | bytes 786436
  315.2 6.6 copy-start.14
  315.2 6.7 copy-start.21
  321.8 12.5 %copy-start.42 = (bf16[12,64,256]{2,1,0:T(8,128)(2,1)}, bf16[12,64,256]{2,1,0:T(8,128)(2,1)S(1)}, u32[]{:S(2)}) copy-start(bf16[12,64,256]{2,1,0:T(8,128)(2,1)S(1)} %fusion.39) | copy-start | bytes 1179652
  321.9 12.5 %slice-start.2 = ((s8[4718592]{0:T(1024)(128)(4,1)}), s8[4194304]{0:T(1024)(128)(4,1)S(1)}, s32[]{:S(2)}) async-start(s8[4718592]{0:T(1024)(128)(4,1)} %bitcast.245), calls=%async_computation.31 | async-start | bytes 8388608
  322.7 11.6 %slice-start.3 = ((s8[4718592]{0:T(1024)(128)(4,1)}), s8[524288]{0:T(1024)(128)(4,1)S(1)}, s32[]{:S(2)}) async-start(s8[4718592]{0:T(1024)(128)(4,1)} %bitcast.245), calls=%async_computation.32 | async-start | bytes 1048576
  360.9 70.7 %reduce-scatter.17.cloned.1.call-start = ((), (), s32[]{:S(2)}) async-start(), calls=%async_computation.14 | async-start | bytes 1966080 | tf_op jit(solution)/shard_map/reduce_scatter | solution.py:194
  367.9 6.4 copy-start.18
  377.5 91.3 %reduce-scatter.23.cloned.1.call-start = ((), (), s32[]{:S(2)}) async-start(), calls=%async_computation.17 | async-start | bytes 1966080 | tf_op jit(solution)/shard_map/reduce_scatter | solution.py:200
  391.4 113.8 %reduce-scatter.21.cloned.1.call-start = ((), (), s32[]{:S(2)}) async-start(), calls=%async_computation.16 | async-start | bytes 1966080 | tf_op jit(solution)/shard_map/reduce_scatter | solution.py:194
  398.6 6.5 copy-start.16
  408.3 141.8 %reduce-scatter.25.cloned.1.call-start = ((), (), s32[]{:S(2)}) async-start(), calls=%async_computation.18 | async-start | bytes 2654208 | tf_op jit(solution)/shard_map/reduce_scatter | solution.py:290
  412.8 206.6 %reduce-scatter.31.cloned.1.call-start = ((), (), s32[]{:S(2)}) async-start(), calls=%async_computation.25 | async-start | bytes 7962624
  413.2 6.2 copy-start.11
  419.4 12.2 %copy-start.22 = (bf16[2,1,256,768]{3,2,1,0:T(8,128)(2,1)S(1)}, bf16[2,1,256,768]{3,2,1,0:T(8,128)(2,1)}, u32[]{:S(2)}) copy-start(bf16[2,1,256,768]{3,2,1,0:T(8,128)(2,1)} %param.11) | copy-start | bytes 2359300
  520.9 178.3 %reduce-scatter.27.cloned.1.call-start = ((), (), s32[]{:S(2)}) async-start(), calls=%async_computation.19 | async-start | bytes 10616832 | tf_op jit(solution)/shard_map/reduce_scatter | solution.py:291
  529.3 249.7 %reduce-scatter.29.cloned.1.call-start = ((), (), s32[]{:S(2)}) async-start(), calls=%async_computation.20 | async-start | bytes 10616832 | tf_op jit(solution)/shard_map/reduce_scatter | solution.py:292
  538.4 278.1 %reduce-scatter.35.cloned.1.call-start = ((), (), s32[]{:S(2)}) async-start(), calls=%async_computation.27 | async-start | bytes 442368
  539.9 313.4 %reduce-scatter.33.cloned.1.call-start = ((), (), s32[]{:S(2)}) async-start(), calls=%async_computation.26 | async-start | bytes 442368
  541.6 396.6 %all-reduce.5.cloned.1.call-start = ((), (), s32[]{:S(2)}) async-start(), calls=%async_computation.28 | async-start | bytes 3833856 | tf_op jit(solution)/shard_map/psum | solution.py:298
  551.7 229.6 %copy-start.53 = (u32[32]{0:T(128)S(1)}, u32[32]{0:T(128)}, u32[]{:S(2)}) copy-start(u32[32]{0:T(128)} %constant.157) | copy-start | bytes 388
  621.6 184.1 %copy-start.34 = (bf16[1,1,256,768]{3,2,1,0:T(8,128)(2,1)S(1)}, bf16[1,1,256,768]{3,2,1,0:T(8,128)(2,1)}, u32[]{:S(2)}) copy-start(bf16[1,1,256,768]{3,2,1,0:T(8,128)(2,1)} %get-tuple-element.112) | copy-start | bytes 1179652
  621.6 184.1 %copy-start.35 = (bf16[1,1,256,768]{3,2,1,0:T(8,128)(2,1)S(1)}, bf16[1,1,256,768]{3,2,1,0:T(8,128)(2,1)}, u32[]{:S(2)}) copy-start(bf16[1,1,256,768]{3,2,1,0:T(8,128)(2,1)} %get-tuple-element.113) | copy-start | bytes 1179652
  701.4 115.9 %copy-start.25 = (f32[256,768]{1,0:T(8,128)S(1)}, f32[256,768]{1,0:T(8,128)}, u32[]{:S(2)}) copy-start(f32[256,768]{1,0:T(8,128)} %get-tuple-element.121) | copy-start | bytes 2359300
  701.4 115.9 %copy-start.33 = (bf16[12,64,256]{2,1,0:T(8,128)(2,1)S(1)}, bf16[12,64,256]{2,1,0:T(8,128)(2,1)}, u32[]{:S(2)}) copy-start(bf16[12,64,256]{2,1,0:T(8,128)(2,1)} %get-tuple-element.147) | copy-start | bytes 1179652
  701.4 115.9 %copy-start.43 = (bf16[1,256,768]{1,2,0:T(8,128)(2,1)S(1)}, bf16[1,256,768]{1,2,0:T(8,128)(2,1)}, u32[]{:S(2)}) copy-start(bf16[1,256,768]{1,2,0:T(8,128)(2,1)} %reduce-scatter.21.cloned.1.call-done) | copy-start | bytes 1179652
  822.0 123.4 %copy-start.1 = (s32[12,16,3]{1,2,0:T(4,128)S(1)}, s32[12,16,3]{1,2,0:T(4,128)}, u32[]{:S(2)}) copy-start(s32[12,16,3]{1,2,0:T(4,128)} %param.14) | copy-start | bytes 6916
  938.2 6.1 copy-start.40
  (32 other events, 92.8 us)
Sparse Core Ops, SparseCore 0:
  10.5 36.6 all-gather.15
  52.8 37.0 all-gather.29
  92.0 35.9 all-gather.27
  129.8 22.9 all-gather.17
  155.0 38.9 all-gather.19
  196.3 38.9 all-gather.21
  237.4 37.0 all-gather.25
  276.6 35.9 all-gather.23
  361.0 34.1 reduce-scatter.18
  397.3 34.2 reduce-scatter.16
  434.5 34.2 reduce-scatter.22
  471.0 34.2 reduce-scatter.20
  508.6 41.4 reduce-scatter.24
  553.9 65.4 reduce-scatter.30
  622.7 76.4 reduce-scatter.26
  702.6 76.4 reduce-scatter.28
  782.6 33.8 reduce-scatter.34
  819.4 33.8 reduce-scatter.32
  856.4 81.6 all-reduce.4
where the time goes:
time: 959 us; the launch traced here: 952 us
  waiting for transfers between devices  597 us (62%)
  matrix products  162 us (17%)
  local copies, waits for them, and re-layouts  64.6 us (7%)
  blocking collectives  60.5 us (6%)
  other arithmetic  50 us (5%)
  between operations  16.1 us (2%)
    unnamed x22, waiting for transfers between devices  108 us
    reduce_scatter x1, waiting for transfers between devices, body(): lax.psum_scatter(totals[3], 'dp', scatter_dimension=0, tiled=True)  77.7 us
    reduce_scatter x1, waiting for transfers between devices, body(): lax.psum_scatter(totals[2], 'dp', scatter_dimension=0, tiled=True)  77.6 us
    psum x1, waiting for transfers between devices, body(): lax.psum(shards[0].astype(jnp.bfloat16), 'seq').astype(jnp.float32)  70.5 us
    reduce_scatter x2, waiting for transfers between devices, backward_pass(): lax.psum_scatter(key_part.reshape(seq_count, seq_len, model_width).astype...  42.9 us
    all_gather x1, waiting for transfers between devices, body(): lax.all_gather(halves[2], 'dp', axis=0, tiled=True)  39.1 us
    all_gather x1, waiting for transfers between devices, body(): lax.all_gather(halves[0], 'dp', axis=0, tiled=True)  37.9 us
    all_gather x2, waiting for transfers between devices, forward_pass(): lax.all_gather(keys_loc.reshape(seq_count, local_rows, model_width), 'seq...  35 us
  transfers between devices with their start and end apart: 19, of which 16 were waited for; matrix products, arithmetic and copies ran while one was open for 22% of the time, Pallas kernels for 0%

commit v1 on v0

--- a/solution.py
+++ b/solution.py
@@ -5,6 +5,34 @@
 
 EPSILON = 1e-05
 MASKED = -1e30
+
+
+def find_map_by_axis(local_block):
+    named_axis = "seq"
+    x_next, q_next, z_new = (
+        lax.axis_size(named_axis),
+        lax.axis_index(named_axis),
+        local_block.shape[1],
+    )
+    entries = list(map(lambda j0: (j0, (j0 + 1) % x_next), range(x_next)))
+    pile = list(map(lambda j0: (j0, (j0 - 1) % x_next), range(x_next)))
+    shaped = jnp.zeros(
+        (*local_block.shape[:1], x_next * z_new, *local_block.shape[2:]), local_block.dtype
+    )
+    local_out = block_now = local_block
+    formed = x_next // 2
+    shaped = lax.dynamic_update_slice_in_dim(shaped, local_block, q_next * z_new, axis=1)
+    for idx in tuple(range(1, formed + 1)):
+        local_out = lax.ppermute(local_out, axis_name=named_axis, perm=entries)
+        shaped = lax.dynamic_update_slice_in_dim(
+            shaped, local_out, (q_next - idx) % x_next * z_new, axis=1
+        )
+        if idx < x_next - formed:
+            block_now = lax.ppermute(block_now, axis_name=named_axis, perm=pile)
+            shaped = lax.dynamic_update_slice_in_dim(
+                shaped, block_now, (q_next + idx) % x_next * z_new, axis=1
+            )
+    return shaped
 
 
 def layer_norm(tensor, gain_row, offset):
@@ -82,9 +110,7 @@
         lax.all_gather(
             keys_loc.reshape(seq_count, local_rows, model_width), "seq", axis=1, tiled=True
         ),
-        lax.all_gather(
-            values_loc.reshape(seq_count, local_rows, model_width), "seq", axis=1, tiled=True
-        ),
+        find_map_by_axis(values_loc.reshape(seq_count, local_rows, model_width)),
     )
     seq_len = keys_full.shape[1]
     query_heads = queries.reshape(seq_count, local_rows, head_count, head_size)

time: 959 us -> 914 us (0.953)
  waiting for transfers between devices: 597 us -> 532 us
  local copies, waits for them, and re-layouts: 64.6 us -> 85.4 us
    all_gather x1, waiting for transfers between devices: 39.1 us -> 4.62 us  [body(): lax.all_gather(halves[2], 'dp', axis=0, tiled=True)]
    all_gather x2 -> x0, waiting for transfers between devices: 24 us -> none  [forward_pass(): lax.all_gather(values_loc.reshape(seq_count, local_rows, model_width), 's...]
    all_gather x1, waiting for transfers between devices: 15 us -> 0.01 us  [body(): lax.all_gather(halves[1], 'dp', axis=0, tiled=True)]
    ppermute x0 -> x6, local copies, waits for them, and re-layouts: none -> 11.5 us  [the longest x4 7.66 us: find_map_by_axis(): local_out = lax.ppermute(local_out, axis_name=named_axis, perm=entries)]
    unnamed x132 -> x136, local copies, waits for them, and re-layouts: 28.7 us -> 31.3 us
    unnamed x22 -> x20, waiting for transfers between devices: 108 us -> 108 us
  transfers between devices with their start and end apart: 19 -> 23, of which waited for: 16 -> 16; matrix products, arithmetic and copies ran while one was open for 22% -> 23% of each run, Pallas kernels for 0% -> 0%
where the time goes in v1:
time: 914 us; the launch traced here: 906 us
  waiting for transfers between devices  532 us (58%)
  matrix products  155 us (17%)
  local copies, waits for them, and re-layouts  85.4 us (9%)
  blocking collectives  60.4 us (7%)
  other arithmetic  48.2 us (5%)
  between operations  16.4 us (2%)
    unnamed x20, waiting for transfers between devices  108 us
    reduce_scatter x1, waiting for transfers between devices, body(): lax.psum_scatter(totals[2], 'dp', scatter_dimension=0, tiled=True)  77.8 us
    reduce_scatter x1, waiting for transfers between devices, body(): lax.psum_scatter(totals[3], 'dp', scatter_dimension=0, tiled=True)  77.7 us
    psum x1, waiting for transfers between devices, body(): lax.psum(shards[0].astype(jnp.bfloat16), 'seq').astype(jnp.float32)  70.4 us
    reduce_scatter x2, waiting for transfers between devices, backward_pass(): lax.psum_scatter(key_part.reshape(seq_count, seq_len, model_width).astype...  43.3 us
    all_gather x1, waiting for transfers between devices, body(): lax.all_gather(halves[0], 'dp', axis=0, tiled=True)  37.9 us
    all_gather x2, waiting for transfers between devices, forward_pass(): lax.all_gather(keys_loc.reshape(seq_count, local_rows, model_width), 'seq...  34 us
    dot_general x8, matrix products, outer_grad(): lax.dot_general(left, right, (((0,), (0,)), ((), ())), preferred_element_...  33.4 us
  transfers between devices with their start and end apart: 23, of which 16 were waited for; matrix products, arithmetic and copies ran while one was open for 23% of the time, Pallas kernels for 0%

profile of v1, /device:TPU:0, one launch (start us, length us, event | category | flops | bytes accessed | tf_op | source)
XLA Modules:
  0.0 905.5 jit_solution(15123889313823833585)
XLA Ops:
  9.3 37.9 %all-gather.12.cloned.1.call-done = bf16[768,2304]{1,0:T(8,128)(2,1)} async-done(((bf16[96,2304]{1,0:T(8,128)(2,1)}), bf16[768,2304]{1,0:T(8,128)(2,1)}) %all-gather.12.cloned.1.call-update) | async-done | bytes 3538960 | tf_op jit(solution)/shard_map/all_gather | solution.py:289
  47.2 3.2 fusion.66
  55.4 8.9 all-gather.2
  64.4 7.8 all-gather.3
  74.7 3.3 fusion.69
  85.4 8.9 all-gather.4
  94.3 4.3 broadcast_in_dim.25
  98.7 17.3 %reshape.625 = pred[12,256,1024]{2,1,0:T(32,128)(4,1)} reshape(pred[12,4,64,16,64]{4,3,2,1,0:T(8,128)(4,1)} %broadcast_in_dim.25) | data formatting | bytes 6291456 | tf_op jit(solution)/shard_map/reshape | solution.py:85
  140.7 5.9 collective-permute-done.2
  153.2 6.4 fusion.102
  164.2 3.8 fusion.38
  170.2 4.6 all-gather.16.cloned.1.call-done
  174.8 11.6 %multiply_convert_fusion.4 = (bf16[256,3072]{1,0:T(8,128)(2,1)}, f32[256,3072]{1,0:T(8,128)}, f32[256,3072]{1,0:T(8,128)}) fusion(f32[3072]{0:T(1024)S(1)} %bitcast.243, bf16[768,3072]{1,0:T(8,128)(2,1)} %all-gather.16.cloned.1.call-done, f32[256,768]{1,0:T(8,128)S(1)} %get-tuple-element.135, f32[256]{0:T(256)S(1)} %fusion.81, ...), kind=kOutput, calls=%fused_computation.37 | convolution fusion | flops 1260847104 | bytes 13389824 | tf_op jit(solution)/shard_map/dot_general | solution.py:137
  186.4 29.6 %all-gather.18.cloned.1.call-done = bf16[3072,768]{1,0:T(8,128)(2,1)} async-done(((bf16[384,768]{1,0:T(8,128)(2,1)}), bf16[3072,768]{1,0:T(8,128)(2,1)}) %all-gather.18.cloned.1.call-update) | async-done | bytes 4718608 | tf_op jit(solution)/shard_map/all_gather | solution.py:292
  216.1 4.3 fusion.104
  220.7 34.0 %all-gather.20.cloned.1.call-done = bf16[1024,768]{1,0:T(8,128)(2,1)} async-done(((bf16[256,768]{1,0:T(8,128)(2,1)}), bf16[1024,768]{1,0:T(8,128)(2,1)}) %all-gather.20.cloned.1.call-update) | async-done | bytes 1572880 | tf_op jit(solution)/shard_map/all_gather | solution.py:110
  257.2 6.7 fusion.99
  266.6 3.5 copy-done.3
  270.2 3.1 fusion.39
  274.2 11.0 %multiply_convert_fusion.5 = (bf16[256,3072]{1,0:T(8,128)(2,1)S(1)}, f32[256,3072]{1,0:T(8,128)}, f32[256,3072]{1,0:T(8,128)}) fusion(f32[3072]{0:T(1024)S(1)} %bitcast.244, bf16[768,3072]{1,0:T(8,128)(2,1)S(1)} %bitcast.248, f32[256,768]{1,0:T(8,128)S(1)} %get-tuple-element.128, f32[768]{0:T(1024)S(1)} %get-tuple-element.70, ...), kind=kOutput, calls=%fused_computation.50 | convolution fusion | flops 1260847104 | bytes 13389824 | tf_op jit(solution)/shard_map/dot_general | solution.py:137
  305.8 8.1 fusion.24
  314.0 7.0 multiply_reduce_fusion.1
  321.0 6.4 multiply_convert_fusion.1
  336.3 8.0 fusion.27
  344.4 7.2 multiply_reduce_fusion
  351.6 6.6 multiply_convert_fusion
  362.9 2.9 convolution_add_fusion.4
  366.1 6.2 convert_reduce_fusion.7
  372.3 5.7 convert_reduce_fusion.11
  378.0 6.9 reduce-scatter.17.cloned.1.call-done
  384.8 5.2 fusion.60
  390.1 31.9 %reduce-scatter.23.cloned.1.call-done = bf16[1,256,768]{1,2,0:T(8,128)(2,1)} async-done(((bf16[1,1024,768]{1,2,0:T(8,128)(2,1)}), bf16[1,256,768]{1,2,0:T(8,128)(2,1)}) %reduce-scatter.23.cloned.1.call-update) | async-done | bytes 393232 | tf_op jit(solution)/shard_map/reduce_scatter | solution.py:226
  422.0 36.4 %reduce-scatter.21.cloned.1.call-done = bf16[1,256,768]{1,2,0:T(8,128)(2,1)} async-done(((bf16[1,1024,768]{1,2,0:T(8,128)(2,1)}), bf16[1,256,768]{1,2,0:T(8,128)(2,1)}) %reduce-scatter.21.cloned.1.call-update) | async-done | bytes 393232 | tf_op jit(solution)/shard_map/reduce_scatter | solution.py:220
  458.5 7.4 add_bitcast_fusion
  465.8 8.2 copy.112
  474.1 3.1 fusion.89
  477.3 5.2 convolution_add_fusion.1
  486.4 5.2 convolution_add_fusion
  494.9 8.4 reduce-scatter.25.cloned.1.call-done
  504.9 67.7 %reduce-scatter.31.cloned.1.call-done = f32[96,2304]{1,0:T(8,128)} async-done(((f32[768,2304]{1,0:T(8,128)}), f32[96,2304]{1,0:T(8,128)}) %reduce-scatter.31.cloned.1.call-update) | async-done | bytes 884752
  574.8 77.8 %reduce-scatter.27.cloned.1.call-done = f32[96,3072]{1,0:T(8,128)} async-done(((f32[768,3072]{1,0:T(8,128)}), f32[96,3072]{1,0:T(8,128)}) %reduce-scatter.27.cloned.1.call-update) | async-done | bytes 1179664 | tf_op jit(solution)/shard_map/reduce_scatter | solution.py:317
  654.8 77.7 %reduce-scatter.29.cloned.1.call-done = f32[384,768]{1,0:T(8,128)} async-done(((f32[3072,768]{1,0:T(8,128)}), f32[384,768]{1,0:T(8,128)}) %reduce-scatter.29.cloned.1.call-update) | async-done | bytes 1179664 | tf_op jit(solution)/shard_map/reduce_scatter | solution.py:318
  735.9 23.1 %all-reduce = bf16[3072]{0:T(1024)(128)(2,1)S(1)} all-reduce(f32[3072]{0:T(1024)S(1)} %add.377), channel_id=12, replica_groups=mesh['dp'=8,'seq'=4] {'dp'}, use_global_device_ids=true, to_apply=%region_37.38.clone | all-reduce | flops 3072 | bytes 18432
  760.1 9.8 %reduce-scatter.35.cloned.1.call-done = f32[96,2]{1,0:T(8,128)} async-done(((f32[768,2]{1,0:T(8,128)}), f32[96,2]{1,0:T(8,128)}) %reduce-scatter.35.cloned.1.call-update) | async-done | bytes 784
  770.8 3.3 fusion.32
  776.6 30.0 %reduce-scatter.33.cloned.1.call-done = f32[96,6]{1,0:T(8,128)} async-done(((f32[768,6]{1,0:T(8,128)}), f32[96,6]{1,0:T(8,128)}) %reduce-scatter.33.cloned.1.call-update) | async-done | bytes 2320
  807.5 11.8 %all-reduce.1 = (bf16[384]{0:T(512)(128)(2,1)S(1)}, bf16[6,96]{1,0:T(8,128)(2,1)S(1)}, bf16[2,96]{1,0:T(2,128)(2,1)S(1)}) all-reduce(bf16[384]{0:T(512)(128)(2,1)S(1)} %dynamic-slice.5, bf16[6,96]{1,0:T(8,128)(2,1)S(1)} %copy.115, bf16[2,96]{1,0:T(2,128)(2,1)S(1)} %copy.117), channel_id=1, replica_groups=mesh['dp'=8,'seq'=4] {'seq'}, use_global_device_ids=true, to_apply=%region_38.39 | all-reduce | flops 1152 | bytes 4608 | tf_op jit(solution)/shard_map/psum | solution.py:328
  821.0 70.4 %all-reduce.5.cloned.1.call-done = (bf16[96,2304]{0,1:T(8,128)(2,1)}, bf16[96,768]{1,0:T(8,128)(2,1)}, bf16[96,3072]{1,0:T(8,128)(2,1)}, bf16[384,768]{1,0:T(8,128)(2,1)}) async-done(((bf16[96,2304]{0,1:T(8,128)(2,1)}, bf16[96,768]{1,0:T(8,128)(2,1)}, bf16[96,3072]{1,0:T(8,128)(2,1)}, bf16[384,768]{1,0:T(8,128)(2,1)}), (bf16[96,2304]{0,1:T(8,128)(2,1)}, bf16[96,768]{1,0:T(8,128)(2,1)}, ...) | async-done | bytes 1769488 | tf_op jit(solution)/shard_map/psum | solution.py:324
  (315 shorter events, 125.5 us)
Async XLA Ops:
  7.2 65.1 %copy-start = (s32[12,16,3]{1,2,0:T(4,128)S(1)}, s32[12,16,3]{1,2,0:T(4,128)}, u32[]{:S(2)}) copy-start(s32[12,16,3]{1,2,0:T(4,128)} %param.14) | copy-start | bytes 6916
  7.2 40.0 %all-gather.12.cloned.1.call-start = ((), (), s32[]{:S(2)}) async-start(), calls=%async_computation.10 | async-start | bytes 3981312 | tf_op jit(solution)/shard_map/all_gather | solution.py:289
  9.2 43.5 %copy-start.48 = (f32[96,768]{1,0:T(8,128)S(1)}, f32[96,768]{1,0:T(8,128)}, u32[]{:S(2)}) copy-start(f32[96,768]{1,0:T(8,128)} %param.16) | copy-start | bytes 884740
  9.3 44.2 %copy-start.42 = (f32[96,3072]{1,0:T(8,128)S(1)}, f32[96,3072]{1,0:T(8,128)}, u32[]{:S(2)}) copy-start(f32[96,3072]{1,0:T(8,128)} %param.17) | copy-start | bytes 3538948
  9.3 141.7 %all-gather.22.cloned.1.call-start = ((), (), s32[]{:S(2)}) async-start(), calls=%async_computation.22 | async-start | bytes 1966080 | tf_op jit(solution)/shard_map/all_gather | solution.py:110
  51.8 12.5 %copy-start.53 = (f32[2,96]{1,0:T(2,128)S(1)}, f32[2,96]{1,0:T(2,128)}, u32[]{:S(2)}) copy-start(f32[2,96]{1,0:T(2,128)} %param.21) | copy-start | bytes 2308
  51.8 20.4 %copy-start.50 = (s32[2,1,1024]{2,1,0:T(1,128)S(1)}, s32[2,1,1024]{2,1,0:T(1,128)}, u32[]{:S(2)}) copy-start(s32[2,1,1024]{2,1,0:T(1,128)} %param.13) | copy-start | bytes 24580
  52.7 22.1 %copy-start.20 = (bf16[2,1,256,768]{3,2,1,0:T(8,128)(2,1)S(1)}, bf16[2,1,256,768]{3,2,1,0:T(8,128)(2,1)}, u32[]{:S(2)}) copy-start(bf16[2,1,256,768]{3,2,1,0:T(8,128)(2,1)} %param.11) | copy-start | bytes 2359300
  52.7 115.3 %all-gather.14.cloned.1.call-start = ((), (), s32[]{:S(2)}) async-start(), calls=%async_computation.11 | async-start | bytes 1327104 | tf_op jit(solution)/shard_map/all_gather | solution.py:290
  53.4 121.4 %all-gather.16.cloned.1.call-start = ((), (), s32[]{:S(2)}) async-start(), calls=%async_computation.12 | async-start | bytes 5308416 | tf_op jit(solution)/shard_map/all_gather | solution.py:291
  54.4 161.7 %all-gather.18.cloned.1.call-start = ((), (), s32[]{:S(2)}) async-start(), calls=%async_computation.13 | async-start | bytes 5308416 | tf_op jit(solution)/shard_map/all_gather | solution.py:292
  55.3 199.3 %all-gather.20.cloned.1.call-start = ((), (), s32[]{:S(2)}) async-start(), calls=%async_computation.21 | async-start | bytes 1966080 | tf_op jit(solution)/shard_map/all_gather | solution.py:110
  78.0 7.4 copy-start.52
  79.3 43.5 %collective-permute-start.3 = (bf16[1,256,768]{2,1,0:T(8,128)(2,1)}, bf16[1,256,768]{2,1,0:T(8,128)(2,1)}, u32[]{:S(2)}, u32[]{:S(2)}) collective-permute-start(bf16[1,256,768]{2,1,0:T(8,128)(2,1)} %get-tuple-element.110), channel_id=1, source_target_pairs={{0,1},{1,2},{2,3},{3,0},{4,5},{5,6},{6,7},{7,4},{8,9},{9,10},{10,1... | collective-permute-start | bytes 1179656 | tf_op jit(solution)/shard_map/ppermute | solution.py:26
  80.8 45.5 %collective-permute-start = (bf16[1,256,768]{2,1,0:T(8,128)(2,1)}, bf16[1,256,768]{2,1,0:T(8,128)(2,1)}, u32[]{:S(2)}, u32[]{:S(2)}) collective-permute-start(bf16[1,256,768]{2,1,0:T(8,128)(2,1)} %get-tuple-element.116), channel_id=1, source_target_pairs={{0,1},{1,2},{2,3},{3,0},{4,5},{5,6},{6,7},{7,4},{8,9},{9,10},{10,1... | collective-permute-start | bytes 1179656 | tf_op jit(solution)/shard_map/ppermute | solution.py:26
  82.4 46.9 %collective-permute-start.4 = (bf16[1,256,768]{2,1,0:T(8,128)(2,1)}, bf16[1,256,768]{2,1,0:T(8,128)(2,1)}, u32[]{:S(2)}, u32[]{:S(2)}) collective-permute-start(bf16[1,256,768]{2,1,0:T(8,128)(2,1)} %get-tuple-element.110), channel_id=1, source_target_pairs={{0,3},{1,0},{2,1},{3,2},{4,7},{5,4},{6,5},{7,6},{8,11},{9,8},{10,9... | collective-permute-start | bytes 1179656 | tf_op jit(solution)/shard_map/ppermute | solution.py:31
  84.8 46.5 %collective-permute-start.1 = (bf16[1,256,768]{2,1,0:T(8,128)(2,1)}, bf16[1,256,768]{2,1,0:T(8,128)(2,1)}, u32[]{:S(2)}, u32[]{:S(2)}) collective-permute-start(bf16[1,256,768]{2,1,0:T(8,128)(2,1)} %get-tuple-element.116), channel_id=1, source_target_pairs={{0,3},{1,0},{2,1},{3,2},{4,7},{5,4},{6,5},{7,6},{8,11},{9,8},{10,9... | collective-permute-start | bytes 1179656 | tf_op jit(solution)/shard_map/ppermute | solution.py:31
  121.7 256.3 %reduce-scatter.19.cloned.1.call-start = ((), (), s32[]{:S(2)}) async-start(), calls=%async_computation.15 | async-start | bytes 1966080 | tf_op jit(solution)/shard_map/reduce_scatter | solution.py:226
  124.7 14.1 %collective-permute-start.5 = (bf16[1,256,768]{2,1,0:T(8,128)(2,1)}, bf16[1,256,768]{2,1,0:T(8,128)(2,1)}, u32[]{:S(2)}, u32[]{:S(2)}) collective-permute-start(bf16[1,256,768]{2,1,0:T(8,128)(2,1)} %collective-permute-done.3), channel_id=1, source_target_pairs={{0,1},{1,2},{2,3},{3,0},{4,5},{5,6},{6,7},{7,4},{8,9},{9,10},{10,1... | collective-permute-start | bytes 1179656 | tf_op jit(solution)/shard_map/ppermute | solution.py:26
  126.2 20.4 %collective-permute-start.2 = (bf16[1,256,768]{2,1,0:T(8,128)(2,1)}, bf16[1,256,768]{2,1,0:T(8,128)(2,1)}, u32[]{:S(2)}, u32[]{:S(2)}) collective-permute-start(bf16[1,256,768]{2,1,0:T(8,128)(2,1)} %collective-permute-done), channel_id=1, source_target_pairs={{0,1},{1,2},{2,3},{3,0},{4,5},{5,6},{6,7},{7,4},{8,9},{9,10},{10,1... | collective-permute-start | bytes 1179656 | tf_op jit(solution)/shard_map/ppermute | solution.py:26
  150.9 11.4 %copy-start.14 = (bf16[1,1024,768]{1,2,0:T(8,128)(2,1)}, bf16[1,1024,768]{1,2,0:T(8,128)(2,1)S(1)}, u32[]{:S(2)}) copy-start(bf16[1,1024,768]{1,2,0:T(8,128)(2,1)S(1)} %get-tuple-element.150) | copy-start | bytes 4718596
  153.2 6.4 copy-start.10
  220.4 36.8 %copy-start.18 = (bf16[256,768]{0,1:T(8,128)(2,1)S(1)}, bf16[256,768]{0,1:T(8,128)(2,1)}, u32[]{:S(2)}) copy-start(bf16[256,768]{0,1:T(8,128)(2,1)} %copy.100) | copy-start | bytes 1179652
  220.4 36.8 %copy-start.49 = (pred[256,1024]{1,0:T(8,128)(4,1)S(1)}, pred[256,1024]{1,0:T(8,128)(4,1)}, u32[]{:S(2)}) copy-start(pred[256,1024]{1,0:T(8,128)(4,1)} %fusion.41) | copy-start | bytes 786436
  263.9 6.2 copy-start.3
  264.0 10.2 %slice-start = ((s8[4718592]{0:T(1024)(128)(4,1)}), s8[4194304]{0:T(1024)(128)(4,1)S(1)}, s32[]{:S(2)}) async-start(s8[4718592]{0:T(1024)(128)(4,1)} %bitcast.247), calls=%async_computation.27 | async-start | bytes 8388608
  273.3 11.9 %slice-start.2 = ((s8[4718592]{0:T(1024)(128)(4,1)}), s8[4194304]{0:T(1024)(128)(4,1)S(1)}, s32[]{:S(2)}) async-start(s8[4718592]{0:T(1024)(128)(4,1)} %bitcast.249), calls=%async_computation.29 | async-start | bytes 8388608
  274.2 11.0 %slice-start.3 = ((s8[4718592]{0:T(1024)(128)(4,1)}), s8[524288]{0:T(1024)(128)(4,1)S(1)}, s32[]{:S(2)}) async-start(s8[4718592]{0:T(1024)(128)(4,1)} %bitcast.249), calls=%async_computation.30 | async-start | bytes 1048576
  313.9 70.9 %reduce-scatter.17.cloned.1.call-start = ((), (), s32[]{:S(2)}) async-start(), calls=%async_computation.14 | async-start | bytes 1966080 | tf_op jit(solution)/shard_map/reduce_scatter | solution.py:220
  320.9 6.4 copy-start.19
  330.5 91.5 %reduce-scatter.23.cloned.1.call-start = ((), (), s32[]{:S(2)}) async-start(), calls=%async_computation.17 | async-start | bytes 1966080 | tf_op jit(solution)/shard_map/reduce_scatter | solution.py:226
  344.3 114.1 %reduce-scatter.21.cloned.1.call-start = ((), (), s32[]{:S(2)}) async-start(), calls=%async_computation.16 | async-start | bytes 1966080 | tf_op jit(solution)/shard_map/reduce_scatter | solution.py:220
  351.6 6.6 copy-start.17
  361.3 141.9 %reduce-scatter.25.cloned.1.call-start = ((), (), s32[]{:S(2)}) async-start(), calls=%async_computation.18 | async-start | bytes 2654208 | tf_op jit(solution)/shard_map/reduce_scatter | solution.py:316
  365.8 206.8 %reduce-scatter.31.cloned.1.call-start = ((), (), s32[]{:S(2)}) async-start(), calls=%async_computation.23 | async-start | bytes 7962624
  372.3 12.5 %copy-start.23 = (bf16[2,1,256,768]{3,2,1,0:T(8,128)(2,1)S(1)}, bf16[2,1,256,768]{3,2,1,0:T(8,128)(2,1)}, u32[]{:S(2)}) copy-start(bf16[2,1,256,768]{3,2,1,0:T(8,128)(2,1)} %param.11) | copy-start | bytes 2359300
  474.1 178.5 %reduce-scatter.27.cloned.1.call-start = ((), (), s32[]{:S(2)}) async-start(), calls=%async_computation.19 | async-start | bytes 10616832 | tf_op jit(solution)/shard_map/reduce_scatter | solution.py:317
  482.6 249.9 %reduce-scatter.29.cloned.1.call-start = ((), (), s32[]{:S(2)}) async-start(), calls=%async_computation.20 | async-start | bytes 10616832 | tf_op jit(solution)/shard_map/reduce_scatter | solution.py:318
  491.6 278.2 %reduce-scatter.35.cloned.1.call-start = ((), (), s32[]{:S(2)}) async-start(), calls=%async_computation.25 | async-start | bytes 442368
  493.1 313.5 %reduce-scatter.33.cloned.1.call-start = ((), (), s32[]{:S(2)}) async-start(), calls=%async_computation.24 | async-start | bytes 442368
  494.9 396.5 %all-reduce.5.cloned.1.call-start = ((), (), s32[]{:S(2)}) async-start(), calls=%async_computation.26 | async-start | bytes 3833856 | tf_op jit(solution)/shard_map/psum | solution.py:324
  504.9 229.8 %copy-start.54 = (u32[32]{0:T(128)S(1)}, u32[32]{0:T(128)}, u32[]{:S(2)}) copy-start(u32[32]{0:T(128)} %constant.190) | copy-start | bytes 388
  574.8 184.3 %copy-start.35 = (bf16[1,1,256,768]{3,2,1,0:T(8,128)(2,1)S(1)}, bf16[1,1,256,768]{3,2,1,0:T(8,128)(2,1)}, u32[]{:S(2)}) copy-start(bf16[1,1,256,768]{3,2,1,0:T(8,128)(2,1)} %get-tuple-element.112) | copy-start | bytes 1179652
  574.8 184.3 %copy-start.36 = (bf16[1,1,256,768]{3,2,1,0:T(8,128)(2,1)S(1)}, bf16[1,1,256,768]{3,2,1,0:T(8,128)(2,1)}, u32[]{:S(2)}) copy-start(bf16[1,1,256,768]{3,2,1,0:T(8,128)(2,1)} %get-tuple-element.113) | copy-start | bytes 1179652
  654.8 115.9 %copy-start.26 = (f32[256,768]{1,0:T(8,128)S(1)}, f32[256,768]{1,0:T(8,128)}, u32[]{:S(2)}) copy-start(f32[256,768]{1,0:T(8,128)} %get-tuple-element.121) | copy-start | bytes 2359300
  654.8 115.9 %copy-start.34 = (bf16[12,64,256]{2,1,0:T(8,128)(2,1)S(1)}, bf16[12,64,256]{2,1,0:T(8,128)(2,1)}, u32[]{:S(2)}) copy-start(bf16[12,64,256]{2,1,0:T(8,128)(2,1)} %get-tuple-element.147) | copy-start | bytes 1179652
  654.8 115.9 %copy-start.47 = (bf16[1,256,768]{1,2,0:T(8,128)(2,1)S(1)}, bf16[1,256,768]{1,2,0:T(8,128)(2,1)}, u32[]{:S(2)}) copy-start(bf16[1,256,768]{1,2,0:T(8,128)(2,1)} %reduce-scatter.21.cloned.1.call-done) | copy-start | bytes 1179652
  775.3 123.2 %copy-start.1 = (s32[12,16,3]{1,2,0:T(4,128)S(1)}, s32[12,16,3]{1,2,0:T(4,128)}, u32[]{:S(2)}) copy-start(s32[12,16,3]{1,2,0:T(4,128)} %param.14) | copy-start | bytes 6916
  (38 other events, 114.7 us)
Sparse Core Ops, SparseCore 0:
  10.5 36.6 all-gather.11
  52.8 56.1 all-gather.21
  110.9 22.6 all-gather.13
  135.9 38.9 all-gather.15
  177.1 38.9 all-gather.17
  217.5 37.0 all-gather.19
  314.0 34.1 reduce-scatter.18
  350.5 34.2 reduce-scatter.16
  387.7 34.2 reduce-scatter.22
  424.2 34.2 reduce-scatter.20
  461.8 41.4 reduce-scatter.24
  507.0 65.4 reduce-scatter.30
  576.1 76.4 reduce-scatter.26
  656.0 76.4 reduce-scatter.28
  736.0 33.8 reduce-scatter.34
  772.7 33.8 reduce-scatter.32
  809.7 81.6 all-reduce.4
